TPU v7x, 256 devices: a whole 4x4x8 slice. The times are simulated.
256 devices in a mesh: rep: 16 (over z, y_hi), ep: 16 (over x, y_lo, core).
Axes of the slice: x: 4, y: 4 (y_hi: 2, y_lo: 2; y = y_hi * 2 + y_lo), z: 8, core: 2. Of those that a mesh axis runs over, the one named last changes fastest.
Arguments:
- tokens: bfloat16 [8192, 7168], P(('rep', 'ep')), may hold values from -6 to 6
- routes: int32 [8192, 2], P(('rep', 'ep')), may hold values from 0 to 7, all different within a row; in each aligned block of 32 rows (0 to 31, 32 to 63, ...) at most 16 rows name the same one
- gates: float32 [8192, 2], P(('rep', 'ep')), may hold values from 0.2 to 1
- gate_weight: bfloat16 [8192, 7168], P('ep', 'rep'), may hold values from -0.0625 to 0.0625
- up_weight: bfloat16 [8192, 7168], P('ep', 'rep'), may hold values from -0.0625 to 0.0625
- down_weight: bfloat16 [8192, 7168], P('ep', 'rep'), may hold values from -0.1875 to 0.1875
Outputs:
- combined: bfloat16 [8192, 7168], P(('rep', 'ep'))
Inputs may be any that keep to these rules, and one draw needn't show every extreme that they name: `routes`: A row names 2 different experts; in each aligned block of 32 rows (the rows of one device) no expert is named by more than 16 rows, a bound that some block reaches.
All inputs are finite; a program needn't handle non-finite values.
Results may differ from a plain program's by a relative error of at most 0.0065.
Values may be sent and summed in bfloat16 or wider, within the bound.
A program may use at most 128 MiB of HBM per device.

v0:
```python
import jax
import jax.numpy as jnp
from jax import lax
from jax.sharding import PartitionSpec as P


def project_rows(rows, gate_rows, up_rows, down_rows):
    gate_part = lax.dot_general(
        rows, gate_rows, (((1,), (1,)), ((), ())), preferred_element_type=jnp.float32
    )
    up_part = lax.dot_general(
        rows, up_rows, (((1,), (1,)), ((), ())), preferred_element_type=jnp.float32
    )
    hidden = (jax.nn.silu(gate_part) * up_part).astype(jnp.bfloat16)
    return jnp.dot(hidden, down_rows, preferred_element_type=jnp.float32)


def per_device(tokens, routes, gates, gate_weight, up_weight, down_weight):
    tok_rows, width_model = tokens.shape
    top_routes = routes.shape[1]
    groups = lax.axis_size("ep")
    experts_held = groups // 2
    capacity = tok_rows // 2
    slot_count = experts_held * capacity
    flat_routes = routes.reshape(-1)
    onehot = (flat_routes[:, None] == jnp.arange(experts_held, dtype=jnp.int32)[None, :]).astype(
        jnp.int32
    )
    before = jnp.cumsum(onehot, axis=0) - onehot
    slot_index = jnp.sum(before * onehot, axis=1)
    position = flat_routes * capacity + slot_index
    select = (position[:, None] == jnp.arange(slot_count, dtype=jnp.int32)[None, :]).reshape(
        tok_rows, top_routes, slot_count
    )
    dispatch_map = jnp.any(select, axis=1).astype(jnp.bfloat16)
    combine_map = jnp.sum(jnp.where(select, gates[:, :, None], 0.0), axis=1)
    buffer = lax.dot_general(
        dispatch_map, tokens, (((0,), (0,)), ((), ())), preferred_element_type=jnp.float32
    )
    buffer = buffer.astype(jnp.bfloat16).reshape(experts_held, capacity, width_model)
    gate_full, up_full, down_full = (
        lax.all_gather(gate_weight, "rep", axis=1, tiled=True),
        lax.all_gather(up_weight, "rep", axis=1, tiled=True),
        lax.all_gather(down_weight, "rep", axis=1, tiled=True),
    )
    outgoing = jnp.repeat(buffer, 2, axis=0)
    arrived = lax.all_to_all(outgoing, "ep", split_axis=0, concat_axis=0, tiled=True)
    partial_value = project_rows(
        arrived.reshape(-1, width_model), gate_full, up_full, down_full
    ).astype(jnp.bfloat16)
    partial_value = partial_value.reshape(groups, capacity, width_model)
    returned = lax.all_to_all(partial_value, "ep", split_axis=0, concat_axis=0, tiled=True)
    paired = returned.reshape(experts_held, 2, capacity, width_model).astype(jnp.float32)
    expert_out = (paired[:, 0] + paired[:, 1]).astype(jnp.bfloat16).reshape(slot_count, width_model)
    combined = jnp.dot(
        combine_map,
        expert_out.astype(jnp.float32),
        precision=lax.Precision.HIGHEST,
        preferred_element_type=jnp.float32,
    )
    return combined.astype(jnp.bfloat16)


def solution(mesh):
    placed = (
        P(("rep", "ep"), None),
        P(("rep", "ep"), None),
        P(("rep", "ep"), None),
        P("ep", "rep"),
        P("ep", "rep"),
        P("ep", "rep"),
    )
    return jax.shard_map(
        per_device, mesh=mesh, in_specs=placed, out_specs=P(("rep", "ep"), None), check_vma=False
    )
```

profile of v0, /device:TPU:1, one launch (start us, length us, event | category | flops | bytes accessed | tf_op | source)
XLA Modules:
  0.0 494.7 jit_solution(4394823316700894333)
XLA Ops:
  6.5 0.0 copy-start
  6.5 0.0 all-gather.4.cloned.1.call-start
  6.5 0.7 all-gather.4.cloned.1.call-update
  7.3 0.0 all-gather.6.cloned.1.call-start
  7.3 0.7 all-gather.6.cloned.1.call-update
  8.0 0.0 all-gather.8.cloned.1.call-start
  8.1 0.7 all-gather.8.cloned.1.call-update
  8.7 0.8 copy.19
  9.5 0.1 eq.29
  9.6 0.1 fusion.9
  9.7 0.1 reduce_window_sum.11
  9.8 0.2 select_reduce_fusion.1
  10.0 0.1 reduce_sum.21
  10.1 0.1 copy.20
  10.2 0.7 multiply_add_fusion
  10.9 0.1 fusion.8
  10.9 0.0 copy-done
  10.9 0.7 convolution_convert_fusion.1
  11.6 0.5 broadcast_in_dim.21
  12.1 53.8 %all_to_all.10 = bf16[16,16,7168]{2,1,0:T(8,128)(2,1)} all-to-all(bf16[16,16,7168]{2,1,0:T(8,128)(2,1)S(1)} %bitcast.19), channel_id=1, replica_groups=mesh['rep'=16,'ep'=16] {'ep'}, dimensions={0} | all-to-all | bytes 7340032 | tf_op jit(solution)/shard_map/all_to_all | solution.py:47
  65.9 103.9 %all-gather.4.cloned.1.call-done = bf16[512,7168]{0,1:T(8,128)(2,1)} async-done(((bf16[512,448]{0,1:T(8,128)(2,1)}), bf16[512,7168]{0,1:T(8,128)(2,1)}) %all-gather.4.cloned.1.call-update) | async-done | bytes 7340048 | tf_op jit(solution)/shard_map/all_gather | solution.py:42
  169.8 6.2 %fusion.11 = f32[256,512]{1,0:T(8,128)S(1)} fusion(bf16[256,7168]{1,0:T(8,128)(2,1)} %bitcast.16, bf16[512,7168]{0,1:T(8,128)(2,1)} %all-gather.4.cloned.1.call-done), kind=kOutput, calls=%fused_computation.21 | convolution fusion | flops 1879048192 | bytes 11534336 | tf_op jit(solution)/shard_map/dot_general | solution.py:8
  176.0 118.7 %all-gather.6.cloned.1.call-done = bf16[512,7168]{0,1:T(8,128)(2,1)} async-done(((bf16[512,448]{0,1:T(8,128)(2,1)}), bf16[512,7168]{0,1:T(8,128)(2,1)}) %all-gather.6.cloned.1.call-update) | async-done | bytes 7340048 | tf_op jit(solution)/shard_map/all_gather | solution.py:43
  294.7 124.9 %all-gather.8.cloned.1.call-done = bf16[512,7168]{0,1:T(8,128)(2,1)} async-done(((bf16[512,448]{0,1:T(8,128)(2,1)}), bf16[512,7168]{0,1:T(8,128)(2,1)}) %all-gather.8.cloned.1.call-update) | async-done | bytes 7340048 | tf_op jit(solution)/shard_map/all_gather | solution.py:44
  419.7 12.1 %convolution_convert_fusion = bf16[256,7168]{1,0:T(8,128)(2,1)} fusion(bf16[512,7168]{0,1:T(8,128)(2,1)} %all-gather.8.cloned.1.call-done, bf16[256,7168]{1,0:T(8,128)(2,1)} %bitcast.17, bf16[512,7168]{0,1:T(8,128)(2,1)} %all-gather.6.cloned.1.call-done, f32[256,512]{1,0:T(8,128)S(1)} %fusion.11), kind=kOutput, calls=%fused_computation | convolution fusion | flops 3760717824 | bytes 22544384 | tf_op jit(solution)/shard_map/dot_general | solution.py:15
  431.7 0.0 copy-start.1
  431.7 5.5 %all-to-all-start.1 = ((bf16[16,16,7168]{2,1,0:T(8,128)(2,1)}), bf16[16,16,7168]{2,1,0:T(8,128)(2,1)}, u32[]{:S(2)}, u32[]{:S(2)}) async-start(bf16[16,16,7168]{2,1,0:T(8,128)(2,1)} %bitcast.18), calls=%async_computation.1 | async-start | bytes 7340032 | tf_op jit(solution)/shard_map/all_to_all | solution.py:52
  437.2 0.0 copy-done.1
  437.2 0.1 select_reduce_fusion
  437.3 45.9 %all-to-all-done.1 = bf16[16,16,7168]{2,1,0:T(8,128)(2,1)} async-done(((bf16[16,16,7168]{2,1,0:T(8,128)(2,1)}), bf16[16,16,7168]{2,1,0:T(8,128)(2,1)}, u32[]{:S(2)}, u32[]{:S(2)}) %all-to-all-start.1) | async-done | bytes 3670048 | tf_op jit(solution)/shard_map/all_to_all | solution.py:52
  483.3 2.9 convert.1
  486.2 0.4 fusion
  486.5 1.6 convolution_convert_fusion.2
Async XLA Ops:
  6.5 4.4 copy-start
  6.5 163.2 %all-gather.4.cloned.1.call-start = ((), (), s32[]{:S(2)}) async-start(), calls=%async_computation.2 | async-start | bytes 7798784 | tf_op jit(solution)/shard_map/all_gather | solution.py:42
  7.3 287.5 %all-gather.6.cloned.1.call-start = ((), (), s32[]{:S(2)}) async-start(), calls=%async_computation.3 | async-start | bytes 7798784 | tf_op jit(solution)/shard_map/all_gather | solution.py:43
  8.0 411.6 %all-gather.8.cloned.1.call-start = ((), (), s32[]{:S(2)}) async-start(), calls=%async_computation.4 | async-start | bytes 7798784 | tf_op jit(solution)/shard_map/all_gather | solution.py:44
  431.7 5.5 %copy-start.1 = (f32[32,2]{0,1:T(2,128)S(1)}, f32[32,2]{0,1:T(2,128)}, u32[]{:S(2)}) copy-start(f32[32,2]{0,1:T(2,128)} %param.8) | copy-start | bytes 772
  431.7 51.5 %all-to-all-start.1 = ((bf16[16,16,7168]{2,1,0:T(8,128)(2,1)}), bf16[16,16,7168]{2,1,0:T(8,128)(2,1)}, u32[]{:S(2)}, u32[]{:S(2)}) async-start(bf16[16,16,7168]{2,1,0:T(8,128)(2,1)} %bitcast.18), calls=%async_computation.1 | async-start | bytes 7340032 | tf_op jit(solution)/shard_map/all_to_all | solution.py:52
Sparse Core Ops, SparseCore 0:
  9.9 159.7 all-gather.3
  172.4 122.3 all-gather.5
  297.3 122.3 all-gather.7
where the time goes:
time: 498 us; the launch traced here: 495 us
  waiting for transfers between devices  396 us (80%)
  blocking collectives  53.8 us (11%)
  matrix products  20.6 us (4%)
  between operations  13.2 us (3%)
  starting transfers between devices  5.58 us (1%)
    all_gather x1, waiting for transfers between devices, per_device(): lax.all_gather(down_weight, 'rep', axis=1, tiled=True)  125 us
    all_gather x1, waiting for transfers between devices, per_device(): lax.all_gather(up_weight, 'rep', axis=1, tiled=True)  119 us
    all_gather x1, waiting for transfers between devices, per_device(): lax.all_gather(gate_weight, 'rep', axis=1, tiled=True)  104 us
    all_to_all x1, blocking collectives, per_device(): lax.all_to_all(outgoing, 'ep', split_axis=0, concat_axis=0, tiled=True)  53.8 us
    all_to_all x1, waiting for transfers between devices, per_device(): lax.all_to_all(partial_value, 'ep', split_axis=0, concat_axis=0, tiled=True)  45.9 us
    dot_general x1, matrix products, project_rows(): return jnp.dot(hidden, down_rows, preferred_element_type=jnp.float32)  12.1 us
  transfers between devices with their start and end apart: 4, of which 4 were waited for; matrix products, arithmetic and copies ran while one was open for 2% of the time, Pallas kernels for 0%

commit v1 on v0

v1 whole, which is shorter than its diff:
```python
import functools

import jax
import jax.numpy as jnp
from jax import lax
from jax.experimental import pallas as pl
from jax.experimental.pallas import tpu as pltpu
from jax.sharding import PartitionSpec as P

F32 = jnp.float32
BF16 = jnp.bfloat16
MESH = pl.DeviceIdType.MESH


def body(
    tokens, routes, gates, gate_w, up_w, down_w, out,
    slots, rows_in, weights, partial_f, partial_tx, partial_rx, hidden,
    half_tx, half_own, half_rx, summed, returned, comb,
    disp_send, disp_recv, disp_local, fwd_sem,
    ring_send, ring_recv, part_sem, half_sem, ret_send, ret_recv, ret_local,
):
    rep, ep = lax.axis_index("rep"), lax.axis_index("ep")
    z, g = rep // 2, rep % 2
    c, q = ep // 2, ep % 2
    mine = g * 8 + c
    hid_rows, width = gate_w.shape
    half_hid = hid_rows // 2
    half_w = width // 2
    cap = 16
    zs = 8

    def rep_of(z_at, g_at):
        return (z_at % zs) * 2 + g_at

    sibling = {"rep": rep, "ep": c * 2 + 1 - q}
    pair = {"rep": z * 2 + 1 - g, "ep": ep}
    up_z = {"rep": rep_of(z + 1, g), "ep": ep}
    down_z = {"rep": rep_of(z + zs - 1, g), "ep": ep}

    def plane(number):
        return {"rep": z * 2 + number // 8, "ep": (number % 8) * 2 + q}

    barrier = pltpu.get_barrier_semaphore()
    for peer in (sibling, up_z, down_z):
        pl.semaphore_signal(barrier, inc=1, device_id=peer, device_id_type=MESH)

    def greet(k, carry):
        pl.semaphore_signal(
            barrier, inc=1, device_id=plane((mine + k) % 16), device_id_type=MESH
        )
        return carry

    lax.fori_loop(1, 16, greet, 0)

    def prepare(chunk):
        if chunk < 2:
            at = chunk * half_hid
            weights[chunk, z, :, 0:half_hid] = gate_w[at : at + half_hid, :].T
            weights[chunk, z, :, half_hid:] = up_w[at : at + half_hid, :].T
        else:
            weights[chunk, z, :, :] = down_w[...].T

    prepare(0)
    pl.semaphore_wait(barrier, 18)

    def ring_copy(chunk, step, direction, half):
        at = (z + zs - (step - 1)) % zs if direction == 0 else (z + step - 1) % zs
        ref = weights.at[chunk, at, pl.ds(half * half_w, half_w), :]
        return pltpu.make_async_remote_copy(
            src_ref=ref, dst_ref=ref,
            send_sem=ring_send.at[chunk, step - 1, direction, half],
            recv_sem=ring_recv.at[chunk, step - 1, direction, half],
            device_id=up_z if direction == 0 else down_z, device_id_type=MESH,
        )

    def ring_arrival(chunk, step, direction, half):
        at = (z + zs - step) % zs if direction == 0 else (z + step) % zs
        ref = weights.at[chunk, at, pl.ds(half * half_w, half_w), :]
        pltpu.make_async_remote_copy(
            src_ref=ref, dst_ref=ref,
            send_sem=ring_send.at[chunk, step - 1, direction, half],
            recv_sem=ring_recv.at[chunk, step - 1, direction, half],
            device_id=up_z if direction == 0 else down_z, device_id_type=MESH,
        ).wait_recv()

    def hops(step):
        if step == 4:
            return ((0, 0), (1, 1))
        return ((0, 0), (1, 1), (0, 1), (1, 0))

    def ring_open(chunk):
        for direction, half in hops(1):
            ring_copy(chunk, 1, direction, half).start()

    def ring_step(chunk, step):
        for direction, half in hops(step):
            ring_arrival(chunk, step, direction, half)
            if step < 3 or (step == 3 and direction == half):
                ring_copy(chunk, step + 1, direction, half).start()

    ring_open(0)

    lane = lax.broadcasted_iota(jnp.int32, (32, 128), 1)
    expert_of, slot_of = lane // cap, lane % cap
    first = routes[:, 0:1] == expert_of
    second = routes[:, 1:2] == expert_of
    named = jnp.where(first | second, 1.0, 0.0).astype(BF16)
    earlier = jnp.where(
        lax.broadcasted_iota(jnp.int32, (32, 32), 1) < lax.broadcasted_iota(jnp.int32, (32, 32), 0),
        1.0, 0.0,
    ).astype(BF16)
    before = jnp.dot(earlier, named, preferred_element_type=F32)
    taken = (first | second) & (before == slot_of.astype(F32))
    send_map = jnp.where(taken, 1.0, 0.0).astype(BF16)
    comb_map = jnp.where(
        taken, jnp.where(first, gates[:, 0:1], 0.0) + jnp.where(second, gates[:, 1:2], 0.0), 0.0
    )
    comb[0] = comb_map.astype(BF16)
    rest = comb_map - comb[0].astype(F32)
    comb[1] = rest.astype(BF16)
    comb[2] = (rest - comb[1].astype(F32)).astype(BF16)

    for a in range(4):
        block = tokens[:, a * 4 * width : (a + 1) * 4 * width]
        for parity in range(2):
            packed = jnp.concatenate(
                [
                    block[:, parity * width : (parity + 1) * width],
                    block[:, (parity + 2) * width : (parity + 3) * width],
                ],
                axis=1,
            )
            slots[parity * 128 : (parity + 1) * 128, a * 2 * width : (a + 1) * 2 * width] = (
                lax.dot_general(
                    send_map, packed, (((0,), (0,)), ((), ())), preferred_element_type=F32
                ).astype(BF16)
            )

    def rows_of(number):
        return pl.ds(pl.multiple_of(number * cap, cap), cap)

    def disp_copy(k):
        to = (mine + k) % 16
        return pltpu.make_async_remote_copy(
            src_ref=slots.at[rows_of(to), :],
            dst_ref=rows_in.at[q, rows_of(mine), :],
            send_sem=disp_send, recv_sem=disp_recv,
            device_id=plane(to), device_id_type=MESH,
        )

    def disp_start(k, carry):
        disp_copy(k).start()
        return carry

    lax.fori_loop(1, 16, disp_start, 0)
    own_rows = pltpu.make_async_copy(
        slots.at[rows_of(mine), :], rows_in.at[q, rows_of(mine), :], disp_local
    )
    own_rows.start()
    prepare(1)
    prepare(2)

    ring_step(0, 1)

    forward = pltpu.make_async_remote_copy(
        src_ref=rows_in.at[q], dst_ref=rows_in.at[q],
        send_sem=fwd_sem.at[0], recv_sem=fwd_sem.at[1],
        device_id=sibling, device_id_type=MESH,
    )

    ring_step(0, 2)
    own_rows.wait()
    arrived = rows_in.at[q, pl.ds(0, 15 * cap), :]
    pltpu.make_async_copy(arrived, arrived, disp_recv).wait()
    forward.start()
    ring_step(0, 3)
    ring_open(1)
    ring_step(0, 4)
    forward.wait_send()
    pltpu.make_async_remote_copy(
        src_ref=rows_in.at[1 - q], dst_ref=rows_in.at[1 - q],
        send_sem=fwd_sem.at[0], recv_sem=fwd_sem.at[1],
        device_id=sibling, device_id_type=MESH,
    ).wait_recv()

    def part_copy(chunk):
        return pltpu.make_async_remote_copy(
            src_ref=partial_tx.at[chunk], dst_ref=partial_rx.at[chunk],
            send_sem=part_sem.at[0, chunk], recv_sem=part_sem.at[1, chunk],
            device_id=pair, device_id_type=MESH,
        )

    def project(chunk):
        for side in range(2):
            def block(a, total):
                cols = pl.ds(pl.multiple_of(a * 2 * width, 128), 2 * width)
                w = weights[chunk, pl.ds(2 * a, 2)].reshape(2 * width, hid_rows)
                return total + jnp.dot(
                    rows_in[side, :, cols], w, preferred_element_type=F32
                )

            total = lax.fori_loop(0, 4, block, jnp.zeros((256, hid_rows), F32))
            partial_f[chunk, side] = total
            partial_tx[chunk, side] = total.astype(BF16)
        part_copy(chunk).start()

    def activate(chunk):
        part_copy(chunk).wait()
        for side in range(2):
            both = partial_f[chunk, side] + partial_rx[chunk, side].astype(F32)
            gate_part, up_part = both[:, :half_hid], both[:, half_hid:]
            hidden[side, :, chunk * half_hid : (chunk + 1) * half_hid] = (
                gate_part / (1.0 + jnp.exp(-gate_part)) * up_part
            ).astype(BF16)

    project(0)
    ring_step(1, 1)
    ring_step(1, 2)
    ring_step(1, 3)
    ring_open(2)
    activate(0)
    ring_step(1, 4)
    project(1)

    sign = 2 * (z % 2) - 1
    pairs = (z // 2, (z // 2 + 4 + sign) % 4, (z // 2 + 4 - sign) % 4, (z // 2 + 2) % 4)

    def half_copy(s):
        return pltpu.make_async_remote_copy(
            src_ref=half_tx.at[s], dst_ref=half_rx.at[s],
            send_sem=half_sem.at[0, s], recv_sem=half_sem.at[1, s],
            device_id=sibling, device_id_type=MESH,
        )

    def ret_copy(s, k):
        to = (mine + k) % 16
        return pltpu.make_async_remote_copy(
            src_ref=summed.at[s, rows_of(to), :],
            dst_ref=returned.at[s, rows_of(mine), :],
            send_sem=ret_send.at[s], recv_sem=ret_recv.at[s],
            device_id=plane(to), device_id_type=MESH,
        )

    def ret_own(s):
        return pltpu.make_async_copy(
            summed.at[s, rows_of(mine), :], returned.at[s, rows_of(mine), :], ret_local.at[s]
        )

    def lower(s):
        w = weights[2, pl.ds(2 * pairs[s], 2)].reshape(2 * width, hid_rows)
        dims = (((1,), (1,)), ((), ()))
        half_tx[s] = lax.dot_general(
            hidden[1 - q], w, dims, preferred_element_type=F32
        ).astype(BF16)
        half_copy(s).start()
        half_own[...] = lax.dot_general(
            hidden[q], w, dims, preferred_element_type=F32
        ).astype(BF16)
        half_copy(s).wait()
        summed[s] = (half_own[...].astype(F32) + half_rx[s].astype(F32)).astype(BF16)

        def send(k, carry):
            ret_copy(s, k).start()
            return carry

        lax.fori_loop(1, 16, send, 0)
        ret_own(s).start()

    ring_step(2, 1)
    ring_step(2, 2)
    ring_step(2, 3)
    activate(1)
    lower(0)
    lower(1)
    lower(2)
    ring_step(2, 4)
    lower(3)

    def finish(s):
        ret_own(s).wait()
        there = returned.at[s, pl.ds(0, 15 * cap), :]
        pltpu.make_async_copy(there, there, ret_recv.at[s]).wait()
        sums = []
        for parity in range(2):
            block = returned[s, parity * 128 : (parity + 1) * 128, :]
            sums.append(
                (
                    jnp.dot(comb[0], block, preferred_element_type=F32)
                    + jnp.dot(comb[1], block, preferred_element_type=F32)
                    + jnp.dot(comb[2], block, preferred_element_type=F32)
                ).astype(BF16)
            )
        whole = jnp.concatenate(
            [sums[0][:, :width], sums[1][:, :width], sums[0][:, width:], sums[1][:, width:]], axis=1
        )
        out[:, pl.ds(pl.multiple_of(pairs[s] * 4 * width, 128), 4 * width)] = whole

    for s in range(4):
        finish(s)

    sent = slots.at[pl.ds(0, 15 * cap), :]
    pltpu.make_async_copy(sent, sent, disp_send).wait()
    for s in range(4):
        sent = summed.at[s, pl.ds(0, 15 * cap), :]
        pltpu.make_async_copy(sent, sent, ret_send.at[s]).wait()
    for chunk in range(3):
        for step in range(1, 5):
            for direction, half in hops(step):
                ring_copy(chunk, step, direction, half).wait_send()


def per_device(tokens, routes, gates, gate_weight, up_weight, down_weight):
    tok_rows, model = tokens.shape
    hid_rows, width = gate_weight.shape
    vmem = pl.BlockSpec(memory_space=pltpu.VMEM)
    dma = pltpu.SemaphoreType.DMA
    return pl.pallas_call(
        body,
        out_shape=jax.ShapeDtypeStruct((tok_rows, model), BF16),
        in_specs=[vmem] * 6,
        out_specs=vmem,
        scratch_shapes=[
            pltpu.VMEM((256, model // 2), BF16),
            pltpu.VMEM((2, 256, model // 2), BF16),
            pltpu.VMEM((3, 8, width, hid_rows), BF16),
            pltpu.VMEM((2, 2, 256, hid_rows), F32),
            pltpu.VMEM((2, 2, 256, hid_rows), BF16),
            pltpu.VMEM((2, 2, 256, hid_rows), BF16),
            pltpu.VMEM((2, 256, hid_rows), BF16),
            pltpu.VMEM((4, 256, 2 * width), BF16),
            pltpu.VMEM((256, 2 * width), BF16),
            pltpu.VMEM((4, 256, 2 * width), BF16),
            pltpu.VMEM((4, 256, 2 * width), BF16),
            pltpu.VMEM((4, 256, 2 * width), BF16),
            pltpu.VMEM((3, 32, 128), BF16),
            dma, dma, dma, dma((2,)),
            dma((3, 4, 2, 2)), dma((3, 4, 2, 2)), dma((2, 2)), dma((2, 4)),
            dma((4,)), dma((4,)), dma((4,)),
        ],
        compiler_params=pltpu.CompilerParams(
            collective_id=0, has_side_effects=True, vmem_limit_bytes=58 << 20
        ),
    )(tokens, routes, gates, gate_weight, up_weight, down_weight)


def solution(mesh):
    placed = (
        P(("rep", "ep"), None),
        P(("rep", "ep"), None),
        P(("rep", "ep"), None),
        P("ep", "rep"),
        P("ep", "rep"),
        P("ep", "rep"),
    )
    return jax.shard_map(
        per_device, mesh=mesh, in_specs=placed, out_specs=P(("rep", "ep"), None), check_vma=False
    )
```

time: 498 us -> 150 us (0.30)
  waiting for transfers between devices: 396 us -> 0 us
  Pallas kernels: 0 us -> 142 us
  blocking collectives: 53.8 us -> 0 us
  matrix products: 20.6 us -> 0 us
  between operations: 13.2 us -> 0.01 us
  local copies, waits for them, and re-layouts: 1.51 us -> 7.99 us
  starting transfers between devices: 5.58 us -> 0 us
    all_gather x3 -> x0, waiting for transfers between devices: 348 us -> none  [the longest x1 125 us: per_device(): lax.all_gather(down_weight, 'rep', axis=1, tiled=True)]
    pallas_call x0 -> x1, Pallas kernels: none -> 142 us  [per_device(): pl.pallas_call(body, out_shape=jax.ShapeDtypeStruct((tok_rows, model), BF...]
    all_to_all x1 -> x0, blocking collectives: 53.8 us -> none  [per_device(): lax.all_to_all(outgoing, 'ep', split_axis=0, concat_axis=0, tiled=True)]
    all_to_all x1 -> x0, waiting for transfers between devices: 45.9 us -> none  [per_device(): lax.all_to_all(partial_value, 'ep', split_axis=0, concat_axis=0, tiled=True)]
    dot_general x4 -> x0, matrix products: 20.6 us -> none  [the longest x1 12.1 us: project_rows(): return jnp.dot(hidden, down_rows, preferred_element_type=jnp.float32)]
    unnamed x5 -> x12, local copies, waits for them, and re-layouts: 0.77 us -> 7.99 us
    all_to_all x1 -> x0, starting transfers between devices: 5.5 us -> none  [per_device(): lax.all_to_all(partial_value, 'ep', split_axis=0, concat_axis=0, tiled=True)]
  transfers between devices with their start and end apart: 4 -> 0, of which waited for: 4 -> 0; matrix products, arithmetic and copies ran while one was open for 2% -> 0% of each run, Pallas kernels for 0% -> 0%
where the time goes in v1:
time: 150 us
  Pallas kernels  142 us (95%)
  local copies, waits for them, and re-layouts  7.99 us (5%)
    pallas_call x1, Pallas kernels, per_device(): pl.pallas_call(body, out_shape=jax.ShapeDtypeStruct((tok_rows, model), BF...  142 us
    unnamed x12, local copies, waits for them, and re-layouts  7.99 us

profile of v1, /device:TPU:1, one launch (start us, length us, event | category | flops | bytes accessed | tf_op | source)
XLA Modules:
  0.0 150.3 jit_solution(531532201212861947)
XLA Ops:
  0.0 0.0 copy-start.2
  0.0 1.4 copy.7.routes
  1.4 0.0 copy-done.2
  1.4 0.7 copy.8.gates
  2.1 0.0 copy-start
  2.1 2.1 %copy.9.gate_w = bf16[512,448]{1,0:T(8,128)(2,1)} copy(bf16[512,448]{0,1:T(8,128)(2,1)} %param.9) | data formatting | bytes 917504 | tf_op args[3]
  4.1 0.0 copy-done
  4.2 0.0 copy-start.1
  4.2 1.0 copy.10.up_w
  5.2 0.0 copy-done.1
  5.2 1.0 copy.11.down_w
  6.2 142.3 %shard_map.64 = bf16[32,7168]{1,0:T(8,128)(2,1)} custom-call(bf16[32,7168]{1,0:T(8,128)(2,1)} %tokens.1, s32[32,2]{1,0:T(8,128)} %copy.7.routes, f32[32,2]{1,0:T(8,128)} %copy.8.gates, bf16[512,448]{1,0:T(8,128)(2,1)} %copy.9.gate_w, bf16[512,448]{1,0:T(8,128)(2,1)} %copy.10.up_w, bf16[512,448]{1,0:T(8,128)(2,1)} %copy.11.down_w), custom_call_target="tpu_custom_call" | custom-call | tf_op jit(solution)/shard_map/pallas_call | solution.py:317
  148.5 1.8 %copy.13 = bf16[32,7168]{1,0:T(8,128)(2,1)} copy(bf16[32,7168]{1,0:T(8,128)(2,1)} %shard_map.64) | data formatting | bytes 917504
Async XLA Ops:
  0.0 1.4 copy-start.2
  2.1 2.1 %copy-start = (bf16[512,448]{0,1:T(8,128)(2,1)S(1)}, bf16[512,448]{0,1:T(8,128)(2,1)}, u32[]{:S(2)}) copy-start(bf16[512,448]{0,1:T(8,128)(2,1)} %param.10) | copy-start | bytes 1376260
  4.2 1.0 copy-start.1

commit v2 on v1

v2 whole, which is shorter than its diff:
```python
import functools

import jax
import jax.numpy as jnp
from jax import lax
from jax.experimental import pallas as pl
from jax.experimental.pallas import tpu as pltpu
from jax.sharding import PartitionSpec as P

F32 = jnp.float32
BF16 = jnp.bfloat16
MESH = pl.DeviceIdType.MESH


HIDS = (384, 128)


def body(
    tokens, routes, gates, gate_w, up_w, down_w, out,
    tok, slots, rows_in, w_first, w_second, w_down, part_f0, part_f1, part_tx0, part_tx1,
    part_rx0, part_rx1, hidden, half_tx, half_own, half_rx, summed, returned, comb,
    load_sem, disp_send, disp_recv, disp_local, fwd_sem,
    ring_send, ring_recv, part_sem, half_sem, ret_send, ret_recv, ret_local,
):
    rep, ep = lax.axis_index("rep"), lax.axis_index("ep")
    z, g = rep // 2, rep % 2
    c, q = ep // 2, ep % 2
    mine = g * 8 + c
    width, hid_rows = gate_w.shape
    half_w = width // 2
    cap = 16
    zs = 8
    chunks = (w_first, w_second, w_down)
    part_f, part_tx, part_rx = (part_f0, part_f1), (part_tx0, part_tx1), (part_rx0, part_rx1)

    def rep_of(z_at, g_at):
        return (z_at % zs) * 2 + g_at

    sibling = {"rep": rep, "ep": c * 2 + 1 - q}
    pair = {"rep": z * 2 + 1 - g, "ep": ep}
    up_z = {"rep": rep_of(z + 1, g), "ep": ep}
    down_z = {"rep": rep_of(z + zs - 1, g), "ep": ep}

    def plane(number):
        return {"rep": z * 2 + number // 8, "ep": (number % 8) * 2 + q}

    first, second = HIDS
    loads = [
        pltpu.make_async_copy(src, dst, load_sem.at[i])
        for i, (src, dst) in enumerate((
            (gate_w.at[:, 0:first], w_first.at[z, :, 0:first]),
            (up_w.at[:, 0:first], w_first.at[z, :, first : 2 * first]),
            (tokens, tok),
            (gate_w.at[:, first:], w_second.at[z, :, 0:second]),
            (up_w.at[:, first:], w_second.at[z, :, second : 2 * second]),
            (down_w, w_down.at[z]),
        ))
    ]
    for load in loads:
        load.start()

    barrier = pltpu.get_barrier_semaphore()
    for peer in (sibling, up_z, down_z):
        pl.semaphore_signal(barrier, inc=1, device_id=peer, device_id_type=MESH)

    def greet(k, carry):
        pl.semaphore_signal(
            barrier, inc=1, device_id=plane((mine + k) % 16), device_id_type=MESH
        )
        return carry

    lax.fori_loop(1, 16, greet, 0)
    loads[0].wait()
    loads[1].wait()
    pl.semaphore_wait(barrier, 18)

    def ring_move(chunk, step, direction, half, at):
        ref = chunks[chunk].at[at, pl.ds(half * half_w, half_w), :]
        return pltpu.make_async_remote_copy(
            src_ref=ref, dst_ref=ref,
            send_sem=ring_send.at[chunk, step - 1, direction, half],
            recv_sem=ring_recv.at[chunk, step - 1, direction, half],
            device_id=up_z if direction == 0 else down_z, device_id_type=MESH,
        )

    def ring_copy(chunk, step, direction, half):
        at = (z + zs - (step - 1)) % zs if direction == 0 else (z + step - 1) % zs
        return ring_move(chunk, step, direction, half, at)

    def ring_arrival(chunk, step, direction, half):
        at = (z + zs - step) % zs if direction == 0 else (z + step) % zs
        ring_move(chunk, step, direction, half, at).wait_recv()

    def hops(step):
        if step == 4:
            return ((0, 0), (1, 1))
        return ((0, 0), (1, 1), (0, 1), (1, 0))

    def ring_open(chunk):
        for direction, half in hops(1):
            ring_copy(chunk, 1, direction, half).start()

    def ring_step(chunk, step):
        for direction, half in hops(step):
            ring_arrival(chunk, step, direction, half)
            if step < 3 or (step == 3 and direction == half):
                ring_copy(chunk, step + 1, direction, half).start()

    ring_open(0)

    slot = lax.broadcasted_iota(jnp.int32, (128, 32), 0)
    expert_of, slot_of = slot // cap, slot % cap
    top = routes[0:1, :] == expert_of
    other = routes[1:2, :] == expert_of
    named = jnp.where(top | other, 1.0, 0.0).astype(BF16)
    earlier = jnp.where(
        lax.broadcasted_iota(jnp.int32, (32, 32), 0) < lax.broadcasted_iota(jnp.int32, (32, 32), 1),
        1.0, 0.0,
    ).astype(BF16)
    before = jnp.dot(named, earlier, preferred_element_type=F32)
    taken = (top | other) & (before == slot_of.astype(F32))
    send_map = jnp.where(taken, 1.0, 0.0).astype(BF16)
    comb_map = jnp.where(
        taken, jnp.where(top, gates[0:1, :], 0.0) + jnp.where(other, gates[1:2, :], 0.0), 0.0
    )
    comb[0] = comb_map.astype(BF16)
    rest = comb_map - comb[0].astype(F32)
    comb[1] = rest.astype(BF16)
    comb[2] = (rest - comb[1].astype(F32)).astype(BF16)

    loads[2].wait()
    for a in range(4):
        block = tok[:, a * 4 * width : (a + 1) * 4 * width]
        for parity in range(2):
            packed = jnp.concatenate(
                [
                    block[:, parity * width : (parity + 1) * width],
                    block[:, (parity + 2) * width : (parity + 3) * width],
                ],
                axis=1,
            )
            slots[parity * 128 : (parity + 1) * 128, a * 2 * width : (a + 1) * 2 * width] = (
                jnp.dot(send_map, packed, preferred_element_type=F32).astype(BF16)
            )

    def rows_of(number):
        return pl.ds(pl.multiple_of(number * cap, cap), cap)

    def disp_copy(k):
        to = (mine + k) % 16
        return pltpu.make_async_remote_copy(
            src_ref=slots.at[rows_of(to), :],
            dst_ref=rows_in.at[q, rows_of(mine), :],
            send_sem=disp_send, recv_sem=disp_recv,
            device_id=plane(to), device_id_type=MESH,
        )

    def disp_start(k, carry):
        disp_copy(k).start()
        return carry

    lax.fori_loop(1, 16, disp_start, 0)
    own_rows = pltpu.make_async_copy(
        slots.at[rows_of(mine), :], rows_in.at[q, rows_of(mine), :], disp_local
    )
    own_rows.start()
    for load in loads[3:]:
        load.wait()

    def forward(side):
        return pltpu.make_async_remote_copy(
            src_ref=rows_in.at[side], dst_ref=rows_in.at[side],
            send_sem=fwd_sem.at[0], recv_sem=fwd_sem.at[1],
            device_id=sibling, device_id_type=MESH,
        )

    def part_copy(chunk):
        return pltpu.make_async_remote_copy(
            src_ref=part_tx[chunk], dst_ref=part_rx[chunk],
            send_sem=part_sem.at[0, chunk], recv_sem=part_sem.at[1, chunk],
            device_id=pair, device_id_type=MESH,
        )

    def project(chunk):
        for side in range(2):
            for a in range(4):
                w = chunks[chunk][2 * a : 2 * a + 2].reshape(2 * width, 2 * HIDS[chunk])
                term = jnp.dot(
                    rows_in[side, :, a * 2 * width : (a + 1) * 2 * width], w,
                    preferred_element_type=F32,
                )
                if a == 0:
                    part_f[chunk][side] = term
                else:
                    part_f[chunk][side] += term
            part_tx[chunk][side] = part_f[chunk][side].astype(BF16)
        part_copy(chunk).start()

    def activate(chunk):
        part_copy(chunk).wait()
        n = HIDS[chunk]
        at = sum(HIDS[:chunk])
        for side in range(2):
            both = part_f[chunk][side] + part_rx[chunk][side].astype(F32)
            gate_part, up_part = both[:, :n], both[:, n:]
            hidden[side, :, at : at + n] = (
                gate_part / (1.0 + jnp.exp(-gate_part)) * up_part
            ).astype(BF16)

    sign = 2 * (z % 2) - 1
    pairs = (z // 2, (z // 2 + 4 + sign) % 4, (z // 2 + 4 - sign) % 4, (z // 2 + 2) % 4)

    def half_copy(s):
        return pltpu.make_async_remote_copy(
            src_ref=half_tx.at[s], dst_ref=half_rx.at[s],
            send_sem=half_sem.at[0, s], recv_sem=half_sem.at[1, s],
            device_id=sibling, device_id_type=MESH,
        )

    def ret_copy(s, k):
        to = (mine + k) % 16
        return pltpu.make_async_remote_copy(
            src_ref=summed.at[s, rows_of(to), :],
            dst_ref=returned.at[s, rows_of(mine), :],
            send_sem=ret_send.at[s], recv_sem=ret_recv.at[s],
            device_id=plane(to), device_id_type=MESH,
        )

    def ret_own(s):
        return pltpu.make_async_copy(
            summed.at[s, rows_of(mine), :], returned.at[s, rows_of(mine), :], ret_local.at[s]
        )

    def lower(s):
        w = w_down[pl.ds(2 * pairs[s], 2)].reshape(2 * width, hid_rows)
        dims = (((1,), (1,)), ((), ()))
        half_tx[s] = lax.dot_general(
            hidden[1 - q], w, dims, preferred_element_type=F32
        ).astype(BF16)
        half_copy(s).start()
        half_own[...] = lax.dot_general(
            hidden[q], w, dims, preferred_element_type=F32
        ).astype(BF16)

    def give_back(s):
        half_copy(s).wait()
        summed[s] = (half_own[...].astype(F32) + half_rx[s].astype(F32)).astype(BF16)

        def send(k, carry):
            ret_copy(s, k).start()
            return carry

        lax.fori_loop(1, 16, send, 0)
        ret_own(s).start()

    def finish(s):
        ret_own(s).wait()
        there = returned.at[s, pl.ds(0, 15 * cap), :]
        pltpu.make_async_copy(there, there, ret_recv.at[s]).wait()
        dims = (((0,), (0,)), ((), ()))
        sums = []
        for parity in range(2):
            block = returned[s, parity * 128 : (parity + 1) * 128, :]
            sums.append(
                (
                    lax.dot_general(comb[0], block, dims, preferred_element_type=F32)
                    + lax.dot_general(comb[1], block, dims, preferred_element_type=F32)
                    + lax.dot_general(comb[2], block, dims, preferred_element_type=F32)
                ).astype(BF16)
            )
        whole = jnp.concatenate(
            [sums[0][:, :width], sums[1][:, :width], sums[0][:, width:], sums[1][:, width:]], axis=1
        )
        out[:, pl.ds(pl.multiple_of(pairs[s] * 4 * width, 128), 4 * width)] = whole

    ring_step(0, 1)
    ring_step(0, 2)
    own_rows.wait()
    arrived = rows_in.at[q, pl.ds(0, 15 * cap), :]
    pltpu.make_async_copy(arrived, arrived, disp_recv).wait()
    forward(q).start()
    ring_step(0, 3)
    ring_open(1)
    ring_step(0, 4)
    forward(q).wait_send()
    forward(1 - q).wait_recv()
    project(0)
    ring_step(1, 1)
    ring_step(1, 2)
    ring_step(1, 3)
    ring_open(2)
    ring_step(1, 4)
    project(1)
    activate(0)
    ring_step(2, 1)
    activate(1)
    lower(0)
    give_back(0)
    ring_step(2, 2)
    lower(1)
    give_back(1)
    finish(0)
    ring_step(2, 3)
    lower(2)
    give_back(2)
    ring_step(2, 4)
    lower(3)
    give_back(3)
    finish(1)
    finish(2)
    finish(3)

    sent = slots.at[pl.ds(0, 15 * cap), :]
    pltpu.make_async_copy(sent, sent, disp_send).wait()
    for s in range(4):
        sent = summed.at[s, pl.ds(0, 15 * cap), :]
        pltpu.make_async_copy(sent, sent, ret_send.at[s]).wait()
    for chunk in range(3):
        for step in range(1, 5):
            for direction, half in hops(step):
                ring_copy(chunk, step, direction, half).wait_send()


def per_device(tokens, routes, gates, gate_weight, up_weight, down_weight):
    tok_rows, model = tokens.shape
    hid_rows, width = gate_weight.shape
    vmem = pl.BlockSpec(memory_space=pltpu.VMEM)
    hbm = pl.BlockSpec(memory_space=pltpu.HBM)
    dma = pltpu.SemaphoreType.DMA
    first, second = HIDS
    return pl.pallas_call(
        body,
        out_shape=jax.ShapeDtypeStruct((tok_rows, model), BF16),
        in_specs=[hbm, vmem, vmem, hbm, hbm, hbm],
        out_specs=vmem,
        scratch_shapes=[
            pltpu.VMEM((tok_rows, model), BF16),
            pltpu.VMEM((256, model // 2), BF16),
            pltpu.VMEM((2, 256, model // 2), BF16),
            pltpu.VMEM((8, width, 2 * first), BF16),
            pltpu.VMEM((8, width, 2 * second), BF16),
            pltpu.VMEM((8, width, hid_rows), BF16),
            pltpu.VMEM((2, 256, 2 * first), F32),
            pltpu.VMEM((2, 256, 2 * second), F32),
            pltpu.VMEM((2, 256, 2 * first), BF16),
            pltpu.VMEM((2, 256, 2 * second), BF16),
            pltpu.VMEM((2, 256, 2 * first), BF16),
            pltpu.VMEM((2, 256, 2 * second), BF16),
            pltpu.VMEM((2, 256, hid_rows), BF16),
            pltpu.VMEM((4, 256, 2 * width), BF16),
            pltpu.VMEM((256, 2 * width), BF16),
            pltpu.VMEM((4, 256, 2 * width), BF16),
            pltpu.VMEM((4, 256, 2 * width), BF16),
            pltpu.VMEM((4, 256, 2 * width), BF16),
            pltpu.VMEM((3, 128, 32), BF16),
            dma((6,)), dma, dma, dma, dma((2,)),
            dma((3, 4, 2, 2)), dma((3, 4, 2, 2)), dma((2, 2)), dma((2, 4)),
            dma((4,)), dma((4,)), dma((4,)),
        ],
        compiler_params=pltpu.CompilerParams(
            collective_id=0, has_side_effects=True, vmem_limit_bytes=56 << 20
        ),
    )(tokens, routes.T, gates.T, gate_weight.T, up_weight.T, down_weight.T)


def solution(mesh):
    placed = (
        P(("rep", "ep"), None),
        P(("rep", "ep"), None),
        P(("rep", "ep"), None),
        P("ep", "rep"),
        P("ep", "rep"),
        P("ep", "rep"),
    )
    return jax.shard_map(
        per_device, mesh=mesh, in_specs=placed, out_specs=P(("rep", "ep"), None), check_vma=False
    )
```

time: 150 us -> 134 us (0.89)
  Pallas kernels: 142 us -> 132 us
  local copies, waits for them, and re-layouts: 7.99 us -> 1.82 us
    pallas_call x1, Pallas kernels: 142 us -> 132 us  [per_device(): pl.pallas_call(body, out_shape=jax.ShapeDtypeStruct((tok_rows, model), BF...]
    unnamed x12 -> x1, local copies, waits for them, and re-layouts: 7.99 us -> 1.82 us
where the time goes in v2:
time: 134 us
  Pallas kernels  132 us (99%)
  local copies, waits for them, and re-layouts  1.82 us (1%)
    pallas_call x1, Pallas kernels, per_device(): pl.pallas_call(body, out_shape=jax.ShapeDtypeStruct((tok_rows, model), BF...  132 us

profile of v2, /device:TPU:1, one launch (start us, length us, event | category | flops | bytes accessed | tf_op | source)
XLA Modules:
  0.0 134.0 jit_solution(18196435871241711196)
XLA Ops:
  0.0 132.1 %shard_map.64 = bf16[32,7168]{1,0:T(8,128)(2,1)} custom-call(bf16[32,7168]{1,0:T(8,128)(2,1)} %tokens.1, s32[2,32]{1,0:T(2,128)} %bitcast.8, f32[2,32]{1,0:T(2,128)} %bitcast.9, bf16[448,512]{1,0:T(8,128)(2,1)} %bitcast.5, bf16[448,512]{1,0:T(8,128)(2,1)} %bitcast.6, bf16[448,512]{1,0:T(8,128)(2,1)} %bitcast.7), custom_call_target="tpu_custom_call" | custom-call | tf_op jit(solution)/shard_map/pallas_call | solution.py:331
  132.1 1.8 %copy.8 = bf16[32,7168]{1,0:T(8,128)(2,1)} copy(bf16[32,7168]{1,0:T(8,128)(2,1)} %shard_map.64) | data formatting | bytes 917504

commit v3 on v2

v3 whole, which is shorter than its diff:
```python
import functools

import jax
import jax.numpy as jnp
from jax import lax
from jax.experimental import pallas as pl
from jax.experimental.pallas import tpu as pltpu
from jax.sharding import PartitionSpec as P

F32 = jnp.float32
BF16 = jnp.bfloat16
MESH = pl.DeviceIdType.MESH


HIDS = (256, 128, 128)
COLS = (320, 128)
AROUND = (
    (2, 2), (-1, 2), (2, -1), (1, 2), (2, 1), (0, 2), (2, 0), (-1, 1), (1, -1), (-1, -1), (1, 1),
    (0, -1), (-1, 0), (0, 1), (1, 0),
)


def body(
    tokens, routes, gates, gate_w, up_w, down_w, out,
    tok, slots, rows_in, w0, w1, w2, w3, w4,
    part_f0, part_f1, part_f2, part_tx0, part_tx1, part_tx2, part_rx0, part_rx1, part_rx2,
    hidden, half_tx_a, half_tx_b, half_own_a, half_own_b, half_rx_a, half_rx_b,
    summed_a, summed_b, returned_a, returned_b, sums_a, comb,
    load_sem, disp_send, disp_recv, disp_local, fwd_sem,
    ring_send, ring_recv, part_sem, half_sem, ret_send, ret_recv, ret_local,
):
    rep, ep = lax.axis_index("rep"), lax.axis_index("ep")
    z, g = rep // 2, rep % 2
    c, q = ep // 2, ep % 2
    mine = g * 8 + c
    width, hid_rows = gate_w.shape
    cap = 16
    zs = 8
    chunks = (w0, w1, w2, w3, w4)
    part_f = (part_f0, part_f1, part_f2)
    part_tx = (part_tx0, part_tx1, part_tx2)
    part_rx = (part_rx0, part_rx1, part_rx2)
    half_tx, half_own, half_rx = (half_tx_a, half_tx_b), (half_own_a, half_own_b), (half_rx_a, half_rx_b)
    summed, returned = (summed_a, summed_b), (returned_a, returned_b)

    def rep_of(z_at, g_at):
        return (z_at % zs) * 2 + g_at

    sibling = {"rep": rep, "ep": c * 2 + 1 - q}
    pair = {"rep": z * 2 + 1 - g, "ep": ep}
    up_z = {"rep": rep_of(z + 1, g), "ep": ep}
    down_z = {"rep": rep_of(z + zs - 1, g), "ep": ep}

    def plane(number):
        return {"rep": z * 2 + number // 8, "ep": (number % 8) * 2 + q}

    moves, at = [], 0
    for chunk, n in enumerate(HIDS):
        moves.append((gate_w.at[:, at : at + n], chunks[chunk].at[z, :, 0:n]))
        moves.append((up_w.at[:, at : at + n], chunks[chunk].at[z, :, n : 2 * n]))
        if chunk == 0:
            moves.append((tokens, tok))
        at += n
    moves.append((down_w.at[0 : COLS[0], :], w3.at[z]))
    moves.append((down_w.at[COLS[0] :, :], w4.at[z]))
    loads = [
        pltpu.make_async_copy(src, dst, load_sem.at[i]) for i, (src, dst) in enumerate(moves)
    ]
    for load in loads:
        load.start()

    barrier = pltpu.get_barrier_semaphore()
    for peer in (sibling, up_z, down_z):
        pl.semaphore_signal(barrier, inc=1, device_id=peer, device_id_type=MESH)

    def greet(k, carry):
        pl.semaphore_signal(
            barrier, inc=1, device_id=plane((mine + k) % 16), device_id_type=MESH
        )
        return carry

    lax.fori_loop(1, 16, greet, 0)
    loads[0].wait()
    loads[1].wait()
    pl.semaphore_wait(barrier, 18)

    def ring_move(chunk, step, direction, half, at):
        half_w = chunks[chunk].shape[1] // 2
        ref = chunks[chunk].at[at, pl.ds(half * half_w, half_w), :]
        return pltpu.make_async_remote_copy(
            src_ref=ref, dst_ref=ref,
            send_sem=ring_send.at[chunk, step - 1, direction, half],
            recv_sem=ring_recv.at[chunk, step - 1, direction, half],
            device_id=up_z if direction == 0 else down_z, device_id_type=MESH,
        )

    def ring_copy(chunk, step, direction, half):
        at = (z + zs - (step - 1)) % zs if direction == 0 else (z + step - 1) % zs
        return ring_move(chunk, step, direction, half, at)

    def ring_arrival(chunk, step, direction, half):
        at = (z + zs - step) % zs if direction == 0 else (z + step) % zs
        ring_move(chunk, step, direction, half, at).wait_recv()

    def hops(step):
        if step == 4:
            return ((0, 0), (1, 1))
        return ((0, 0), (1, 1), (0, 1), (1, 0))

    def ring_step(chunk, step):
        for direction, half in hops(step):
            ring_arrival(chunk, step, direction, half)
            if step < 3 or (step == 3 and direction == half):
                ring_copy(chunk, step + 1, direction, half).start()
            if step == 3 and chunk < len(chunks) - 1:
                ring_copy(chunk + 1, 1, direction, half).start()

    for direction, half in hops(1):
        ring_copy(0, 1, direction, half).start()

    slot = lax.broadcasted_iota(jnp.int32, (128, 32), 0)
    expert_of, slot_of = slot // cap, slot % cap
    top = routes[0:1, :] == expert_of
    other = routes[1:2, :] == expert_of
    named = jnp.where(top | other, 1.0, 0.0).astype(BF16)
    earlier = jnp.where(
        lax.broadcasted_iota(jnp.int32, (32, 32), 0) < lax.broadcasted_iota(jnp.int32, (32, 32), 1),
        1.0, 0.0,
    ).astype(BF16)
    before = jnp.dot(named, earlier, preferred_element_type=F32)
    taken = (top | other) & (before == slot_of.astype(F32))
    send_map = jnp.where(taken, 1.0, 0.0).astype(BF16)
    comb_map = jnp.where(
        taken, jnp.where(top, gates[0:1, :], 0.0) + jnp.where(other, gates[1:2, :], 0.0), 0.0
    )
    high = comb_map.astype(BF16)
    rest = comb_map - high.astype(F32)
    middle = rest.astype(BF16)
    low = (rest - middle.astype(F32)).astype(BF16)
    comb[...] = jnp.concatenate([high, middle, low], axis=1)

    loads[2].wait()
    for a in range(4):
        block = tok[:, a * 4 * width : (a + 1) * 4 * width]
        for parity in range(2):
            packed = jnp.concatenate(
                [
                    block[:, parity * width : (parity + 1) * width],
                    block[:, (parity + 2) * width : (parity + 3) * width],
                ],
                axis=1,
            )
            slots[parity * 128 : (parity + 1) * 128, a * 2 * width : (a + 1) * 2 * width] = (
                jnp.dot(send_map, packed, preferred_element_type=F32).astype(BF16)
            )

    def rows_of(number):
        return pl.ds(pl.multiple_of(number * cap, cap), cap)

    flip = 1 - 2 * q

    def around(dx, dy):
        x_to = (c // 2 + 4 + dx * flip) % 4
        y_to = (g * 2 + c % 2 + 4 + dy * flip) % 4
        return (y_to // 2) * 8 + x_to * 2 + y_to % 2

    for dx, dy in AROUND:
        to = around(dx, dy)
        pltpu.make_async_remote_copy(
            src_ref=slots.at[rows_of(to), :],
            dst_ref=rows_in.at[q, rows_of(mine), :],
            send_sem=disp_send, recv_sem=disp_recv,
            device_id=plane(to), device_id_type=MESH,
        ).start()
    own_rows = pltpu.make_async_copy(
        slots.at[rows_of(mine), :], rows_in.at[q, rows_of(mine), :], disp_local
    )
    own_rows.start()
    for load in loads[3:]:
        load.wait()

    def forward(side):
        return pltpu.make_async_remote_copy(
            src_ref=rows_in.at[side], dst_ref=rows_in.at[side],
            send_sem=fwd_sem.at[0], recv_sem=fwd_sem.at[1],
            device_id=sibling, device_id_type=MESH,
        )

    def part_copy(chunk):
        return pltpu.make_async_remote_copy(
            src_ref=part_tx[chunk], dst_ref=part_rx[chunk],
            send_sem=part_sem.at[0, chunk], recv_sem=part_sem.at[1, chunk],
            device_id=pair, device_id_type=MESH,
        )

    def project(chunk):
        for side in range(2):
            for a in range(4):
                w = chunks[chunk][2 * a : 2 * a + 2].reshape(2 * width, 2 * HIDS[chunk])
                term = jnp.dot(
                    rows_in[side, :, a * 2 * width : (a + 1) * 2 * width], w,
                    preferred_element_type=F32,
                )
                if a == 0:
                    part_f[chunk][side] = term
                else:
                    part_f[chunk][side] += term
            part_tx[chunk][side] = part_f[chunk][side].astype(BF16)
        part_copy(chunk).start()

    def activate(chunk):
        part_copy(chunk).wait()
        n = HIDS[chunk]
        at = sum(HIDS[:chunk])
        for side in range(2):
            both = part_f[chunk][side] + part_rx[chunk][side].astype(F32)
            gate_part, up_part = both[:, :n], both[:, n:]
            hidden[side, :, at : at + n] = (
                gate_part / (1.0 + jnp.exp(-gate_part)) * up_part
            ).astype(BF16)

    sign = 2 * (z % 2) - 1
    pairs = (z // 2, (z // 2 + 4 + sign) % 4, (z // 2 + 4 - sign) % 4, (z // 2 + 2) % 4)

    def half_copy(kind, s):
        return pltpu.make_async_remote_copy(
            src_ref=half_tx[kind].at[s], dst_ref=half_rx[kind].at[s],
            send_sem=half_sem.at[0, kind, s], recv_sem=half_sem.at[1, kind, s],
            device_id=sibling, device_id_type=MESH,
        )

    def ret_own(kind, s):
        return pltpu.make_async_copy(
            summed[kind].at[s, rows_of(mine), :], returned[kind].at[s, rows_of(mine), :],
            ret_local.at[kind, s],
        )

    def lower(kind, s):
        w = chunks[3 + kind][pl.ds(2 * pairs[s], 2)].reshape(2 * COLS[kind], hid_rows)
        dims = (((1,), (1,)), ((), ()))
        half_tx[kind][s] = lax.dot_general(
            hidden[1 - q], w, dims, preferred_element_type=F32
        ).astype(BF16)
        half_copy(kind, s).start()
        half_own[kind][s] = lax.dot_general(
            hidden[q], w, dims, preferred_element_type=F32
        ).astype(BF16)

    def give_back(kind, s):
        half_copy(kind, s).wait()
        summed[kind][s] = (
            half_own[kind][s].astype(F32) + half_rx[kind][s].astype(F32)
        ).astype(BF16)
        for dx, dy in AROUND:
            to = around(dx, dy)
            pltpu.make_async_remote_copy(
                src_ref=summed[kind].at[s, rows_of(to), :],
                dst_ref=returned[kind].at[s, rows_of(mine), :],
                send_sem=ret_send.at[kind, s], recv_sem=ret_recv.at[kind, s],
                device_id=plane(to), device_id_type=MESH,
            ).start()
        ret_own(kind, s).start()

    def combine(kind, s):
        ret_own(kind, s).wait()
        there = returned[kind].at[s, pl.ds(0, 15 * cap), :]
        pltpu.make_async_copy(there, there, ret_recv.at[kind, s]).wait()
        dims = (((0,), (0,)), ((), ()))
        sums = []
        for parity in range(2):
            block = returned[kind][s, parity * 128 : (parity + 1) * 128, :]
            terms = lax.dot_general(comb[...], block, dims, preferred_element_type=F32)
            sums.append((terms[0:32] + terms[32:64] + terms[64:96]).astype(BF16))
        return sums

    def finish_a(s):
        for parity, value in enumerate(combine(0, s)):
            sums_a[s, parity] = value

    def finish_b(s):
        wide, narrow = COLS
        pieces = combine(1, s)
        whole = []
        for which in range(2):
            for parity in range(2):
                whole.append(sums_a[s, parity, :, which * wide : (which + 1) * wide])
                whole.append(pieces[parity][:, which * narrow : (which + 1) * narrow])
        out[:, pl.ds(pl.multiple_of(pairs[s] * 4 * width, 128), 4 * width)] = jnp.concatenate(
            whole, axis=1
        )

    ring_step(0, 1)
    ring_step(0, 2)
    own_rows.wait()
    arrived = rows_in.at[q, pl.ds(0, 15 * cap), :]
    pltpu.make_async_copy(arrived, arrived, disp_recv).wait()
    forward(q).start()
    ring_step(0, 3)
    ring_step(0, 4)
    forward(q).wait_send()
    forward(1 - q).wait_recv()
    project(0)
    ring_step(1, 1)
    ring_step(1, 2)
    ring_step(1, 3)
    ring_step(1, 4)
    project(1)
    activate(0)
    ring_step(2, 1)
    ring_step(2, 2)
    activate(1)
    ring_step(2, 3)
    ring_step(2, 4)
    project(2)
    ring_step(3, 1)
    activate(2)
    lower(0, 0)
    give_back(0, 0)
    ring_step(3, 2)
    lower(0, 1)
    give_back(0, 1)
    ring_step(3, 3)
    lower(0, 2)
    ring_step(3, 4)
    give_back(0, 2)
    lower(0, 3)
    ring_step(4, 1)
    give_back(0, 3)
    ring_step(4, 2)
    lower(1, 0)
    lower(1, 1)
    finish_a(0)
    give_back(1, 0)
    give_back(1, 1)
    ring_step(4, 3)
    lower(1, 2)
    finish_a(1)
    give_back(1, 2)
    ring_step(4, 4)
    lower(1, 3)
    finish_a(2)
    give_back(1, 3)
    finish_a(3)
    for s in range(4):
        finish_b(s)

    sent = slots.at[pl.ds(0, 15 * cap), :]
    pltpu.make_async_copy(sent, sent, disp_send).wait()
    for kind in range(2):
        for s in range(4):
            sent = summed[kind].at[s, pl.ds(0, 15 * cap), :]
            pltpu.make_async_copy(sent, sent, ret_send.at[kind, s]).wait()
    for chunk in range(5):
        for step in range(1, 5):
            for direction, half in hops(step):
                ring_copy(chunk, step, direction, half).wait_send()


def per_device(tokens, routes, gates, gate_weight, up_weight, down_weight):
    tok_rows, model = tokens.shape
    hid_rows, width = gate_weight.shape
    vmem = pl.BlockSpec(memory_space=pltpu.VMEM)
    hbm = pl.BlockSpec(memory_space=pltpu.HBM)
    dma = pltpu.SemaphoreType.DMA
    halves = [pltpu.VMEM((4, 256, 2 * n), BF16) for n in COLS]
    return pl.pallas_call(
        body,
        out_shape=jax.ShapeDtypeStruct((tok_rows, model), BF16),
        in_specs=[hbm, vmem, vmem, hbm, hbm, hbm],
        out_specs=vmem,
        scratch_shapes=[
            pltpu.VMEM((tok_rows, model), BF16),
            pltpu.VMEM((256, model // 2), BF16),
            pltpu.VMEM((2, 256, model // 2), BF16),
            *[pltpu.VMEM((8, width, 2 * n), BF16) for n in HIDS],
            *[pltpu.VMEM((8, n, hid_rows), BF16) for n in COLS],
            *[pltpu.VMEM((2, 256, 2 * n), F32) for n in HIDS],
            *[pltpu.VMEM((2, 256, 2 * n), BF16) for n in HIDS],
            *[pltpu.VMEM((2, 256, 2 * n), BF16) for n in HIDS],
            pltpu.VMEM((2, 256, hid_rows), BF16),
            *halves,
            *halves,
            *halves,
            *halves,
            *halves,
            pltpu.VMEM((4, 2, tok_rows, 2 * COLS[0]), BF16),
            pltpu.VMEM((128, 96), BF16),
            dma((9,)), dma, dma, dma, dma((2,)),
            dma((5, 4, 2, 2)), dma((5, 4, 2, 2)), dma((2, 3)), dma((2, 2, 4)),
            dma((2, 4)), dma((2, 4)), dma((2, 4)),
        ],
        compiler_params=pltpu.CompilerParams(
            collective_id=0, has_side_effects=True, vmem_limit_bytes=54592 << 10
        ),
    )(tokens, routes.T, gates.T, gate_weight.T, up_weight.T, down_weight.T)


def solution(mesh):
    placed = (
        P(("rep", "ep"), None),
        P(("rep", "ep"), None),
        P(("rep", "ep"), None),
        P("ep", "rep"),
        P("ep", "rep"),
        P("ep", "rep"),
    )
    return jax.shard_map(
        per_device, mesh=mesh, in_specs=placed, out_specs=P(("rep", "ep"), None), check_vma=False
    )
```

time: 134 us -> 131 us (0.978)
  Pallas kernels: 132 us -> 130 us
    pallas_call x1, Pallas kernels: 132 us -> 130 us  [per_device(): pl.pallas_call(body, out_shape=jax.ShapeDtypeStruct((tok_rows, model), BF...]
where the time goes in v3:
time: 131 us
  Pallas kernels  130 us (99%)
  local copies, waits for them, and re-layouts  1.46 us (1%)
    pallas_call x1, Pallas kernels, per_device(): pl.pallas_call(body, out_shape=jax.ShapeDtypeStruct((tok_rows, model), BF...  130 us

profile of v3, /device:TPU:1, one launch (start us, length us, event | category | flops | bytes accessed | tf_op | source)
XLA Modules:
  0.0 131.4 jit_solution(14180500415725074546)
XLA Ops:
  0.0 0.0 copy-start.1
  0.0 0.0 copy-start
  0.0 0.7 copy-done.1
  0.7 0.0 copy-done
  0.7 129.9 %shard_map.64 = bf16[32,7168]{1,0:T(8,128)(2,1)S(1)} custom-call(bf16[32,7168]{1,0:T(8,128)(2,1)} %tokens.1, s32[2,32]{1,0:T(2,128)S(1)} %bitcast.5, f32[2,32]{1,0:T(2,128)S(1)} %bitcast.6, bf16[448,512]{1,0:T(8,128)(2,1)} %bitcast.7, bf16[448,512]{1,0:T(8,128)(2,1)} %bitcast.8, bf16[448,512]{1,0:T(8,128)(2,1)} %bitcast.9), custom_call_target="tpu_custom_call" | custom-call | tf_op jit(solution)/shard_map/pallas_call | solution.py:366
  130.6 0.8 copy.8
Async XLA Ops:
  0.0 0.7 copy-start.1
  0.0 0.7 copy-start

commit v4 on v3

--- a/solution.py
+++ b/solution.py
@@ -48,8 +48,9 @@
 
     sibling = {"rep": rep, "ep": c * 2 + 1 - q}
     pair = {"rep": z * 2 + 1 - g, "ep": ep}
-    up_z = {"rep": rep_of(z + 1, g), "ep": ep}
-    down_z = {"rep": rep_of(z + zs - 1, g), "ep": ep}
+    flip = 1 - 2 * q
+    up_z = {"rep": rep_of(z + zs + flip, g), "ep": ep}
+    down_z = {"rep": rep_of(z + zs - flip, g), "ep": ep}
 
     def plane(number):
         return {"rep": z * 2 + number // 8, "ep": (number % 8) * 2 + q}
@@ -95,11 +96,11 @@
         )
 
     def ring_copy(chunk, step, direction, half):
-        at = (z + zs - (step - 1)) % zs if direction == 0 else (z + step - 1) % zs
+        at = (z + zs + (2 * direction - 1) * flip * (step - 1)) % zs
         return ring_move(chunk, step, direction, half, at)
 
     def ring_arrival(chunk, step, direction, half):
-        at = (z + zs - step) % zs if direction == 0 else (z + step) % zs
+        at = (z + zs + (2 * direction - 1) * flip * step) % zs
         ring_move(chunk, step, direction, half, at).wait_recv()
 
     def hops(step):
@@ -156,8 +157,6 @@
 
     def rows_of(number):
         return pl.ds(pl.multiple_of(number * cap, cap), cap)
-
-    flip = 1 - 2 * q
 
     def around(dx, dy):
         x_to = (c // 2 + 4 + dx * flip) % 4
@@ -329,17 +328,17 @@
     ring_step(4, 2)
     lower(1, 0)
     lower(1, 1)
-    finish_a(0)
+    ring_step(4, 3)
     give_back(1, 0)
     give_back(1, 1)
-    ring_step(4, 3)
     lower(1, 2)
-    finish_a(1)
-    give_back(1, 2)
     ring_step(4, 4)
     lower(1, 3)
+    finish_a(0)
+    give_back(1, 2)
+    finish_a(1)
+    give_back(1, 3)
     finish_a(2)
-    give_back(1, 3)
     finish_a(3)
     for s in range(4):
         finish_b(s)

time: 131 us -> 129 us (0.985)
  Pallas kernels: 130 us -> 128 us
    pallas_call x1, Pallas kernels: 130 us -> 128 us  [per_device(): pl.pallas_call(body, out_shape=jax.ShapeDtypeStruct((tok_rows, model), BF...]
where the time goes in v4:
time: 129 us
  Pallas kernels  128 us (99%)
  local copies, waits for them, and re-layouts  1.46 us (1%)
    pallas_call x1, Pallas kernels, per_device(): pl.pallas_call(body, out_shape=jax.ShapeDtypeStruct((tok_rows, model), BF...  128 us

profile of v4, /device:TPU:1, one launch (start us, length us, event | category | flops | bytes accessed | tf_op | source)
XLA Modules:
  0.0 129.2 jit_solution(10059821345661700768)
XLA Ops:
  0.0 0.0 copy-start.1
  0.0 0.0 copy-start
  0.0 0.7 copy-done.1
  0.7 0.0 copy-done
  0.7 127.8 %shard_map.64 = bf16[32,7168]{1,0:T(8,128)(2,1)S(1)} custom-call(bf16[32,7168]{1,0:T(8,128)(2,1)} %tokens.1, s32[2,32]{1,0:T(2,128)S(1)} %bitcast.5, f32[2,32]{1,0:T(2,128)S(1)} %bitcast.6, bf16[448,512]{1,0:T(8,128)(2,1)} %bitcast.7, bf16[448,512]{1,0:T(8,128)(2,1)} %bitcast.8, bf16[448,512]{1,0:T(8,128)(2,1)} %bitcast.9), custom_call_target="tpu_custom_call" | custom-call | tf_op jit(solution)/shard_map/pallas_call | solution.py:365
  128.5 0.8 copy.8
Async XLA Ops:
  0.0 0.7 copy-start.1
  0.0 0.7 copy-start

commit v5 on v4

--- a/solution.py
+++ b/solution.py
@@ -67,8 +67,8 @@
     loads = [
         pltpu.make_async_copy(src, dst, load_sem.at[i]) for i, (src, dst) in enumerate(moves)
     ]
-    for load in loads:
-        load.start()
+    loads[0].start()
+    loads[1].start()
 
     barrier = pltpu.get_barrier_semaphore()
     for peer in (sibling, up_z, down_z):
@@ -81,6 +81,8 @@
         return carry
 
     lax.fori_loop(1, 16, greet, 0)
+    for load in loads[2:]:
+        load.start()
     loads[0].wait()
     loads[1].wait()
     pl.semaphore_wait(barrier, 18)
@@ -288,6 +290,15 @@
             whole, axis=1
         )
 
+    def ring_sent(chunk):
+        for step in range(1, 5):
+            for direction, half in hops(step):
+                ring_copy(chunk, step, direction, half).wait_send()
+
+    def ret_sent(kind, s):
+        sent = summed[kind].at[s, pl.ds(0, 15 * cap), :]
+        pltpu.make_async_copy(sent, sent, ret_send.at[kind, s]).wait()
+
     ring_step(0, 1)
     ring_step(0, 2)
     own_rows.wait()
@@ -298,6 +309,8 @@
     ring_step(0, 4)
     forward(q).wait_send()
     forward(1 - q).wait_recv()
+    sent = slots.at[pl.ds(0, 15 * cap), :]
+    pltpu.make_async_copy(sent, sent, disp_send).wait()
     project(0)
     ring_step(1, 1)
     ring_step(1, 2)
@@ -305,9 +318,11 @@
     ring_step(1, 4)
     project(1)
     activate(0)
+    ring_sent(0)
     ring_step(2, 1)
     ring_step(2, 2)
     activate(1)
+    ring_sent(1)
     ring_step(2, 3)
     ring_step(2, 4)
     project(2)
@@ -315,9 +330,11 @@
     activate(2)
     lower(0, 0)
     give_back(0, 0)
+    ring_sent(2)
     ring_step(3, 2)
     lower(0, 1)
     give_back(0, 1)
+    finish_a(0)
     ring_step(3, 3)
     lower(0, 2)
     ring_step(3, 4)
@@ -325,34 +342,30 @@
     lower(0, 3)
     ring_step(4, 1)
     give_back(0, 3)
+    lower(1, 0)
     ring_step(4, 2)
-    lower(1, 0)
+    give_back(1, 0)
     lower(1, 1)
     ring_step(4, 3)
-    give_back(1, 0)
     give_back(1, 1)
     lower(1, 2)
     ring_step(4, 4)
     lower(1, 3)
-    finish_a(0)
     give_back(1, 2)
+    give_back(1, 3)
     finish_a(1)
-    give_back(1, 3)
     finish_a(2)
     finish_a(3)
+    ring_sent(3)
     for s in range(4):
-        finish_b(s)
-
-    sent = slots.at[pl.ds(0, 15 * cap), :]
-    pltpu.make_async_copy(sent, sent, disp_send).wait()
-    for kind in range(2):
-        for s in range(4):
-            sent = summed[kind].at[s, pl.ds(0, 15 * cap), :]
-            pltpu.make_async_copy(sent, sent, ret_send.at[kind, s]).wait()
-    for chunk in range(5):
-        for step in range(1, 5):
-            for direction, half in hops(step):
-                ring_copy(chunk, step, direction, half).wait_send()
+        ret_sent(0, s)
+    finish_b(0)
+    finish_b(1)
+    finish_b(2)
+    ring_sent(4)
+    for s in range(4):
+        ret_sent(1, s)
+    finish_b(3)
 
 
 def per_device(tokens, routes, gates, gate_weight, up_weight, down_weight):

time: 129 us -> 129 us (level)
  no operation moved by 1% of the time
where the time goes in v5:
time: 129 us
  Pallas kernels  128 us (99%)
  local copies, waits for them, and re-layouts  1.46 us (1%)
    pallas_call x1, Pallas kernels, per_device(): pl.pallas_call(body, out_shape=jax.ShapeDtypeStruct((tok_rows, model), BF...  128 us

profile of v5, /device:TPU:1, one launch (start us, length us, event | category | flops | bytes accessed | tf_op | source)
XLA Modules:
  0.0 129.0 jit_solution(16606967426762378683)
XLA Ops:
  0.0 0.0 copy-start.1
  0.0 0.0 copy-start
  0.0 0.7 copy-done.1
  0.7 0.0 copy-done
  0.7 127.5 %shard_map.64 = bf16[32,7168]{1,0:T(8,128)(2,1)S(1)} custom-call(bf16[32,7168]{1,0:T(8,128)(2,1)} %tokens.1, s32[2,32]{1,0:T(2,128)S(1)} %bitcast.5, f32[2,32]{1,0:T(2,128)S(1)} %bitcast.6, bf16[448,512]{1,0:T(8,128)(2,1)} %bitcast.7, bf16[448,512]{1,0:T(8,128)(2,1)} %bitcast.8, bf16[448,512]{1,0:T(8,128)(2,1)} %bitcast.9), custom_call_target="tpu_custom_call" | custom-call | tf_op jit(solution)/shard_map/pallas_call | solution.py:378
  128.2 0.8 copy.8
Async XLA Ops:
  0.0 0.7 copy-start.1
  0.0 0.7 copy-start

commit v6 on v5

--- a/solution.py
+++ b/solution.py
@@ -236,16 +236,23 @@
             ret_local.at[kind, s],
         )
 
-    def lower(kind, s):
+    def block(kind, s, side):
         w = chunks[3 + kind][pl.ds(2 * pairs[s], 2)].reshape(2 * COLS[kind], hid_rows)
         dims = (((1,), (1,)), ((), ()))
-        half_tx[kind][s] = lax.dot_general(
-            hidden[1 - q], w, dims, preferred_element_type=F32
+        return lax.dot_general(
+            hidden[side], w, dims, preferred_element_type=F32
         ).astype(BF16)
+
+    def lower_other(kind, s):
+        half_tx[kind][s] = block(kind, s, 1 - q)
         half_copy(kind, s).start()
-        half_own[kind][s] = lax.dot_general(
-            hidden[q], w, dims, preferred_element_type=F32
-        ).astype(BF16)
+
+    def lower_own(kind, s):
+        half_own[kind][s] = block(kind, s, q)
+
+    def lower(kind, s):
+        lower_other(kind, s)
+        lower_own(kind, s)
 
     def give_back(kind, s):
         half_copy(kind, s).wait()
@@ -338,20 +345,25 @@
     ring_step(3, 3)
     lower(0, 2)
     ring_step(3, 4)
+    lower_other(0, 3)
     give_back(0, 2)
-    lower(0, 3)
+    lower_own(0, 3)
     ring_step(4, 1)
+    lower_other(1, 0)
     give_back(0, 3)
-    lower(1, 0)
+    lower_own(1, 0)
     ring_step(4, 2)
+    lower_other(1, 1)
     give_back(1, 0)
-    lower(1, 1)
+    lower_own(1, 1)
     ring_step(4, 3)
+    lower_other(1, 2)
     give_back(1, 1)
-    lower(1, 2)
+    lower_own(1, 2)
     ring_step(4, 4)
-    lower(1, 3)
+    lower_other(1, 3)
     give_back(1, 2)
+    lower_own(1, 3)
     give_back(1, 3)
     finish_a(1)
     finish_a(2)

time: 129 us -> 129 us (level)
  no operation moved by 1% of the time
where the time goes in v6:
time: 129 us
  Pallas kernels  127 us (98%)
  local copies, waits for them, and re-layouts  1.46 us (1%)
    pallas_call x1, Pallas kernels, per_device(): pl.pallas_call(body, out_shape=jax.ShapeDtypeStruct((tok_rows, model), BF...  127 us

profile of v6, /device:TPU:1, one launch (start us, length us, event | category | flops | bytes accessed | tf_op | source)
XLA Modules:
  0.0 128.9 jit_solution(11196747833410691427)
XLA Ops:
  0.0 0.0 copy-start.1
  0.0 0.0 copy-start
  0.0 0.7 copy-done.1
  0.7 0.0 copy-done
  0.7 127.4 %shard_map.64 = bf16[32,7168]{1,0:T(8,128)(2,1)S(1)} custom-call(bf16[32,7168]{1,0:T(8,128)(2,1)} %tokens.1, s32[2,32]{1,0:T(2,128)S(1)} %bitcast.5, f32[2,32]{1,0:T(2,128)S(1)} %bitcast.6, bf16[448,512]{1,0:T(8,128)(2,1)} %bitcast.7, bf16[448,512]{1,0:T(8,128)(2,1)} %bitcast.8, bf16[448,512]{1,0:T(8,128)(2,1)} %bitcast.9), custom_call_target="tpu_custom_call" | custom-call | tf_op jit(solution)/shard_map/pallas_call | solution.py:390
  128.1 0.8 copy.8
Async XLA Ops:
  0.0 0.7 copy-start.1
  0.0 0.7 copy-start
